TPU v7x, 256 devices: a whole 4x4x8 slice. The times are simulated.
256 devices in a mesh: ctx: 32 (over z, x_lo, core), mp: 8 (over y, x_hi).
Axes of the slice: x: 4 (x_hi: 2, x_lo: 2; x = x_hi * 2 + x_lo), y: 4, z: 8, core: 2. Of those that a mesh axis runs over, the one named last changes fastest.
Arguments:
- byte_qkv: bfloat16 [16384, 3, 4096], P('ctx', None, 'mp'), may hold values from -14 to 14
- kv_weight: bfloat16 [4096, 2, 4096], P(None, None, 'mp'), may hold values from -4 to 4
- patch_bounds: int32 [32, 161], replicated, may hold values from 0 to 16384, as said below
Outputs:
- mixed: bfloat16 [5120, 4096], P('ctx', 'mp')
Inputs may be any that keep to these rules, and one draw needn't show every extreme that they name: `patch_bounds`: row c lists in increasing order the first bytes of the patches that begin in bytes c * 512 to (c + 1) * 512 - 1, then the end of its last patch, repeated to the end of the row. The patches cover all 16384 bytes, each is 1 to 16 bytes long, one is exactly 16 long, and some row lists exactly 160 patches.
All inputs are finite; a program needn't handle non-finite values.
Results may differ from a plain program's by a relative error of at most 0.002.
The roundings to bfloat16 on the way count: a program that leaves them out, or rounds other values in their place, can miss the bound.
Values may be sent and summed in bfloat16 or wider, within the bound.
A program may use at most 128 MiB of HBM per device.

v0:
```python
import math

import jax
import jax.numpy as jnp
from jax import lax
from jax.sharding import PartitionSpec as P

D = 4096
HEADS = 32
WIN = 16


masked_score = -1e30


def passed_along(value, axis, steps):
    count = lax.axis_size(axis)
    initial, last = (max(0, -steps), min(count, count - steps))
    return lax.ppermute(value, axis, [(source, source + steps) for source in range(initial, last)])


def shards(byte_qkv, kv_weight, patch_bounds):
    byte_rows = byte_qkv.shape[0]
    col_width = byte_qkv.shape[2]
    head_dim = D // HEADS
    heads_here = col_width // head_dim
    slot_count = patch_bounds.shape[1] - 1
    score_scale = 1.0 / math.sqrt(head_dim)
    ctx_place = lax.axis_index("ctx")
    my_bounds = lax.dynamic_index_in_dim(patch_bounds, ctx_place, 0, keepdims=False)
    starts = my_bounds[:slot_count]
    lengths = my_bounds[1:] - starts
    live_slot = lengths > 0
    edge_rows = passed_along(byte_qkv[:WIN], "ctx", -1)
    extended = jnp.concatenate([byte_qkv, edge_rows], axis=0)
    offsets = jnp.arange(WIN, dtype=jnp.int32)
    local_start = jnp.clip(starts - ctx_place * byte_rows, 0, byte_rows)
    window = extended[local_start[:, None] + offsets[None, :]]
    window = window.reshape(slot_count, WIN, 3, heads_here, head_dim)
    inside = offsets[None, :] < lengths[:, None]
    queries = jnp.max(jnp.where(inside[:, :, None, None], window[:, :, 0], -jnp.inf), axis=1)
    queries = jnp.where(live_slot[:, None, None], queries, 0)
    scores = (
        jnp.einsum("shd,swhd->shw", queries, window[:, :, 1], preferred_element_type=jnp.float32)
        * score_scale
    )
    scores = jnp.where(inside[:, None, :], scores, masked_score)
    scores = scores - jnp.max(scores, axis=2, keepdims=True)
    exp_terms = jnp.exp(scores)
    weights = (exp_terms / jnp.sum(exp_terms, axis=2, keepdims=True)).astype(jnp.bfloat16)
    pooled = jnp.einsum(
        "shw,swhd->shd", weights, window[:, :, 2], preferred_element_type=jnp.float32
    )
    patch_state = (
        jnp.where(live_slot[:, None, None], pooled, 0.0)
        .astype(jnp.bfloat16)
        .reshape(slot_count, col_width)
    )
    flat_weight = kv_weight.reshape(kv_weight.shape[0], 2 * col_width)
    projected = jnp.dot(
        lax.all_gather(patch_state, "mp", axis=1, tiled=True),
        flat_weight,
        preferred_element_type=jnp.float32,
    )
    key_value = projected.astype(jnp.bfloat16)
    query_heads = patch_state.reshape(slot_count, heads_here, head_dim)
    query_slot = ctx_place * slot_count + jnp.arange(slot_count, dtype=jnp.int32)
    valid_all = (patch_bounds[:, 1:] > patch_bounds[:, :-1]).reshape(-1)
    shard_piece = lax.all_gather(key_value, "ctx", axis=0, tiled=True)
    top_score = jnp.full((heads_here, slot_count), masked_score, jnp.float32)
    piece_rows = shard_piece.shape[0]
    key_part = shard_piece[:, :col_width].reshape(piece_rows, heads_here, head_dim)
    value_part = shard_piece[:, col_width:].reshape(piece_rows, heads_here, head_dim)
    key_slot = jnp.arange(piece_rows, dtype=jnp.int32)
    visible = (key_slot[None, :] <= query_slot[:, None]) & valid_all[None, :]
    global_scores = (
        jnp.einsum("qhd,khd->hqk", query_heads, key_part, preferred_element_type=jnp.float32)
        * score_scale
    )
    global_scores = jnp.where(visible[None], global_scores, masked_score)
    new_top = jnp.maximum(top_score, jnp.max(global_scores, axis=2))
    exp_part = jnp.where(visible[None], jnp.exp(global_scores - new_top[:, :, None]), 0.0)
    denom_sum = jnp.sum(exp_part, axis=2)
    weighted = jnp.einsum(
        "hqk,khd->hqd", exp_part, value_part.astype(jnp.float32), precision=lax.Precision.HIGHEST
    )
    fold_state = (new_top, denom_sum, weighted)
    top_score, denom_sum, weighted = fold_state
    safe_total = jnp.where(denom_sum > 0, denom_sum, 1.0)
    attended = (weighted / safe_total[:, :, None]).transpose(1, 0, 2).reshape(slot_count, col_width)
    attended = jnp.where(live_slot[:, None], attended, 0.0)
    return (patch_state.astype(jnp.float32) + attended).astype(jnp.bfloat16)


def solution(mesh):
    return jax.shard_map(
        shards,
        mesh=mesh,
        in_specs=(P("ctx", None, "mp"), P(None, None, "mp"), P()),
        out_specs=P("ctx", "mp"),
        check_vma=False,
    )
```

profile of v0, /device:TPU:1, one launch (start us, length us, event | category | flops | bytes accessed | tf_op | source)
XLA Modules:
  0.0 252.5 jit_solution(9994078554285454188)
XLA Ops:
  6.5 2.8 %copy.29 = bf16[512,3,512]{2,1,0:T(4,128)(2,1)S(1)} copy(bf16[512,3,512]{2,0,1:T(8,128)(2,1)} %param.3) | data formatting | bytes 3145728 | tf_op args[0]
  9.3 1.3 copy-done
  10.7 5.1 %collective-permute-start = (bf16[16,3,512]{2,1,0:T(4,128)(2,1)S(1)}, bf16[16,3,512]{2,1,0:T(4,128)(2,1)S(1)}, u32[]{:S(2)}, u32[]{:S(2)}) collective-permute-start(bf16[16,3,512]{2,1,0:T(4,128)(2,1)S(1)} %slice.44), channel_id=1, source_target_pairs={{8,0},{16,8},{24,16},{32,24},{40,32},{48,40},{56,48},{64,56},{72,6... | collective-permute-start | bytes 147464 | tf_op jit(solution)/shard_map/ppermute | solution.py:19
  15.8 0.9 dynamic-slice_subtract_fusion
  17.1 3.0 %pad_maximum_fusion = bf16[528,3,512]{2,1,0:T(4,128)(2,1)S(1)} fusion(bf16[16,3,512]{2,1,0:T(4,128)(2,1)S(1)} %collective-permute-done, bf16[512,3,512]{2,1,0:T(4,128)(2,1)} %copy-done), kind=kLoop, calls=%fused_computation.31 | loop fusion | flops 811008 | bytes 3244032 | tf_op jit(solution)/shard_map/concatenate | solution.py:35
  20.1 12.8 %gather_fusion = bf16[2560,3,512]{2,1,0:T(4,128)(2,1)} fusion(bf16[528,3,512]{2,1,0:T(4,128)(2,1)S(1)} %pad_maximum_fusion, s32[3072]{0:T(1024)S(1)} %pad_clamp_fusion), kind=kCustom, calls=%fused_computation | custom fusion | bytes 15738880 | tf_op jit(solution)/shard_map/gather | solution.py:38
  33.0 21.7 %reshape.205 = bf16[160,16,3,4,128]{4,3,2,1,0:T(4,128)(2,1)} reshape(bf16[2560,3,512]{2,1,0:T(4,128)(2,1)} %gather_fusion) | data formatting | bytes 15728640 | tf_op jit(solution)/shard_map/reshape | solution.py:39
  54.6 5.4 %fusion.17 = bf16[160,4,128]{2,1,0:T(4,128)(2,1)S(1)} fusion(bf16[160,16,3,4,128]{4,3,2,1,0:T(4,128)(2,1)} %reshape.205, pred[160,16]{1,0:T(8,128)(4,1)S(1)} %iota_compare_fusion.1), kind=kLoop, calls=%fused_computation.26 | loop fusion | flops 2539520 | bytes 2787840 | tf_op jit(solution)/shard_map/reduce_max | solution.py:41
  60.0 5.2 %slice_bitcast_fusion.2 = (bf16[160,16,4,128]{3,2,1,0:T(4,128)(2,1)S(1)}, bf16[160,16,4,128]{3,2,1,0:T(4,128)(2,1)S(1)}) fusion(bf16[160,16,3,4,128]{4,3,2,1,0:T(4,128)(2,1)} %reshape.205), kind=kLoop, calls=%fused_computation.22 | loop fusion | bytes 10485760 | tf_op jit(solution)/shard_map/squeeze | solution.py:52
  65.1 0.2 select_bitcast_fusion
  65.4 1.4 fusion.20
  67.3 0.8 fusion.18
  68.1 0.2 select_convert_fusion
  68.4 0.7 copy.80
  69.3 9.3 %copy.49 = bf16[512,8,2,512]{3,1,2,0:T(8,128)(2,1)} copy(bf16[512,8,2,512]{3,2,1,0:T(2,128)(2,1)} %bitcast.80) | data formatting | bytes 16777216
  78.6 44.9 %all-gather.3.cloned.1.call-done = bf16[160,4096]{1,0:T(8,128)(2,1)} async-done(((bf16[160,512]{1,0:T(8,128)(2,1)}), bf16[160,4096]{1,0:T(8,128)(2,1)}) %all-gather.3.cloned.1.call-update) | async-done | bytes 1310736 | tf_op jit(solution)/shard_map/all_gather | solution.py:61
  123.5 6.1 %convolution_convert_fusion = bf16[160,1024]{1,0:T(8,128)(2,1)} fusion(bf16[160,4096]{1,0:T(8,128)(2,1)} %all-gather.3.cloned.1.call-done, bf16[4096,1024]{1,0:T(8,128)(2,1)} %bitcast.81), kind=kOutput, calls=%fused_computation.32 | convolution fusion | flops 1342341120 | bytes 10027008 | tf_op jit(solution)/shard_map/dot_general | solution.py:60
  129.8 0.6 fusion.15
  130.4 73.0 %all-gather.5.cloned.1.call-done = bf16[5120,1024]{1,0:T(8,128)(2,1)} async-done(((bf16[160,1024]{1,0:T(8,128)(2,1)}), bf16[5120,1024]{1,0:T(8,128)(2,1)}) %all-gather.5.cloned.1.call-update) | async-done | bytes 10485776 | tf_op jit(solution)/shard_map/all_gather | solution.py:69
  203.4 9.7 %slice_bitcast_fusion.1 = (bf16[640,4,8,128]{3,2,1,0:T(8,128)(2,1)}, bf16[640,4,8,128]{3,2,1,0:T(8,128)(2,1)}) fusion(bf16[5120,1024]{1,0:T(8,128)(2,1)} %all-gather.5.cloned.1.call-done), kind=kLoop, calls=%fused_computation.19 | loop fusion | bytes 20971520
  213.1 10.3 %fusion.2 = (f32[4,160]{1,0:T(4,128)S(1)}, f32[4,160,5120]{2,1,0:T(8,128)}) fusion(pred[160,5120]{1,0:T(8,128)(4,1)S(1)} %fusion.15, bf16[640,4,8,128]{3,2,1,0:T(8,128)(2,1)} %get-tuple-element.5, bf16[160,4,128]{2,1,0:T(4,128)(2,1)S(1)} %select_convert_fusion), kind=kOutput, calls=%fused_computation.5 | convolution fusion | flops 848690560 | bytes 19335680 | tf_op jit(solution)/shard_map/qhd,khd->hqk/dot_general | solution.py:77
  223.4 8.8 %fusion.3 = f32[4,160]{1,0:T(4,128)S(1)} fusion(f32[4,160,5120]{2,1,0:T(8,128)} %get-tuple-element.12, f32[4,160]{1,0:T(4,128)S(1)} %broadcast_maximum_fusion, pred[160,5120]{1,0:T(8,128)(4,1)S(1)} %fusion.15), kind=kLoop, calls=%fused_computation.6 | loop fusion | flops 16383360 | bytes 13931520 | tf_op jit(solution)/shard_map/reduce_sum | solution.py:83
  232.3 12.6 %fusion.33 = f32[4,20,8,128]{3,2,1,0:T(8,128)S(1)} fusion(bf16[640,4,8,128]{3,2,1,0:T(8,128)(2,1)} %get-tuple-element.6, f32[4,160,5120]{2,1,0:T(8,128)} %get-tuple-element.12, f32[4,160]{1,0:T(4,128)S(1)} %broadcast_maximum_fusion, pred[160,5120]{1,0:T(8,128)(4,1)S(1)} %fusion.15, f32[160,4]{0,1:T(4,128)S(1)} %compare_select_fusion.1), kind=kOutput, calls=%fused_computation.40 | convolution fusion | flops 5046353920 | bytes 19502080 | tf_op jit(solution)/shard_map/hqk,khd->hqd/dot_general | solution.py:84
  244.9 0.8 fusion.37
  (23 shorter events, 1.4 us)
Async XLA Ops:
  6.5 117.0 %all-gather.3.cloned.1.call-start = ((), (), s32[]{:S(2)}) async-start(), calls=%async_computation | async-start | bytes 1474560 | tf_op jit(solution)/shard_map/all_gather | solution.py:61
  9.3 1.4 copy-start
  10.7 6.4 %collective-permute-start = (bf16[16,3,512]{2,1,0:T(4,128)(2,1)S(1)}, bf16[16,3,512]{2,1,0:T(4,128)(2,1)S(1)}, u32[]{:S(2)}, u32[]{:S(2)}) collective-permute-start(bf16[16,3,512]{2,1,0:T(4,128)(2,1)S(1)} %slice.44), channel_id=1, source_target_pairs={{8,0},{16,8},{24,16},{32,24},{40,32},{48,40},{56,48},{64,56},{72,6... | collective-permute-start | bytes 147464 | tf_op jit(solution)/shard_map/ppermute | solution.py:19
  69.1 134.3 %all-gather.5.cloned.1.call-start = ((), (), s32[]{:S(2)}) async-start(), calls=%async_computation.1 | async-start | bytes 10813440 | tf_op jit(solution)/shard_map/all_gather | solution.py:69
  123.5 6.1 %copy-start.1 = (s32[32,161]{1,0:T(8,128)S(1)}, s32[32,161]{1,0:T(8,128)}, u32[]{:S(2)}) copy-start(s32[32,161]{1,0:T(8,128)} %param.5) | copy-start | bytes 61828
Sparse Core Ops, SparseCore 0:
  69.2 54.2 all-gather.2
  129.7 73.6 all-gather.4
where the time goes:
time: 253 us
  waiting for transfers between devices  118 us (47%)
  local copies, waits for them, and re-layouts  64.2 us (25%)
  matrix products  31.2 us (12%)
  other arithmetic  20.3 us (8%)
  between operations  13.6 us (5%)
  starting transfers between devices  5.33 us (2%)
    all_gather x1, waiting for transfers between devices, shards(): shard_piece = lax.all_gather(key_value, 'ctx', axis=0, tiled=True)  73 us
    all_gather x1, waiting for transfers between devices, shards(): lax.all_gather(patch_state, 'mp', axis=1, tiled=True)  44.9 us
    unnamed x8, local copies, waits for them, and re-layouts  23.8 us
    reshape x1, local copies, waits for them, and re-layouts, shards(): window = window.reshape(slot_count, WIN, 3, heads_here, head_dim)  21.7 us
    gather x1, local copies, waits for them, and re-layouts, shards(): window = extended[local_start[:, None] + offsets[None, :]]  12.8 us
    dot_general x1, matrix products, shards(): jnp.einsum('hqk,khd->hqd', exp_part, value_part.astype(jnp.float32), prec...  12.6 us
    dot_general x1, matrix products, shards(): jnp.einsum('qhd,khd->hqk', query_heads, key_part, preferred_element_type=...  10.3 us
    reduce_sum x1, other arithmetic, shards(): denom_sum = jnp.sum(exp_part, axis=2)  8.85 us
  transfers between devices with their start and end apart: 3, of which 3 were waited for; matrix products, arithmetic and copies ran while one was open for 4% of the time, Pallas kernels for 0%

commit v1 on v0

v1 whole, which is shorter than its diff:
```python
import functools
import math

import jax
import jax.numpy as jnp
from jax import lax
from jax.experimental import pallas as pl
from jax.experimental.pallas import tpu as pltpu
from jax.sharding import PartitionSpec as P

D = 4096
HEADS = 32
WIN = 16
HD = 128
BYTE_DEV = 512
EXT = BYTE_DEV + WIN
PCAP = 160
COLS = 512
HERE = 4
N_MP = 8
N_Z = 8
GROUP = 4
ROWS = GROUP * PCAP
SCALE = 1.0 / math.sqrt(HD)
MASKED = -1e30
F32 = jnp.float32
BF16 = jnp.bfloat16
MESH = pl.DeviceIdType.MESH


def cross_body(bounds_ref, bytes_ref, edge_ref, out_ref, ext):
    c = lax.axis_index("ctx")
    row = bounds_ref[pl.ds(c, 1), :] - c * BYTE_DEV
    starts = row[:, :PCAP]
    ends = row[:, 1 : PCAP + 1]
    diag = lax.broadcasted_iota(jnp.int32, (PCAP, PCAP), 0) == lax.broadcasted_iota(
        jnp.int32, (PCAP, PCAP), 1
    )
    start_col = jnp.sum(jnp.where(diag, starts, 0), axis=1, keepdims=True)
    end_col = jnp.sum(jnp.where(diag, ends, 0), axis=1, keepdims=True)
    byte_row = lax.broadcasted_iota(jnp.int32, (PCAP, EXT), 1)
    inside = (byte_row >= start_col) & (byte_row < end_col)
    first = ((byte_row == start_col) & (end_col > start_col)).astype(F32).astype(BF16)
    byte_col = lax.broadcasted_iota(jnp.int32, (EXT, PCAP), 0)
    inside_t = (byte_col >= starts) & (byte_col < ends)
    left = jnp.sum(jnp.where(inside_t, ends - byte_col, 0), axis=1, keepdims=True)
    for part in range(3):
        ext[part, 0:BYTE_DEV, :] = bytes_ref[part]
        ext[part, BYTE_DEV:EXT, :] = edge_ref[part]
    for h in range(HERE):
        cols = slice(h * HD, (h + 1) * HD)
        top = ext[0, :, cols].astype(F32)
        for shift in (1, 2, 4, 8):
            later = pltpu.roll(top, EXT - shift, 0)
            top = jnp.maximum(top, jnp.where(left > shift, later, -jnp.inf))
        query = jnp.dot(first, top.astype(BF16), preferred_element_type=F32).astype(BF16)
        scores = (
            lax.dot_general(
                query, ext[1, :, cols], (((1,), (1,)), ((), ())), preferred_element_type=F32
            )
            * SCALE
        )
        scores = jnp.where(inside, scores, MASKED)
        scores = scores - jnp.max(scores, axis=1, keepdims=True)
        exp_terms = jnp.where(inside, jnp.exp(scores), 0.0)
        total = jnp.sum(exp_terms, axis=1, keepdims=True)
        weights = (exp_terms / jnp.where(total > 0, total, 1.0)).astype(BF16)
        out_ref[:, cols] = jnp.dot(weights, ext[2, :, cols], preferred_element_type=F32).astype(BF16)


def cross(bounds, bytes3, edge):
    vmem = pl.BlockSpec(memory_space=pltpu.VMEM)
    return pl.pallas_call(
        cross_body,
        out_shape=jax.ShapeDtypeStruct((PCAP, COLS), BF16),
        in_specs=[vmem, vmem, vmem],
        out_specs=vmem,
        scratch_shapes=[pltpu.VMEM((3, EXT, COLS), BF16)],
        compiler_params=pltpu.CompilerParams(vmem_limit_bytes=16 * 2**20),
        name="cross",
    )(bounds, bytes3, edge)


def remote(src, dst, send, recv, where):
    return pltpu.make_async_remote_copy(
        src_ref=src, dst_ref=dst, send_sem=send, recv_sem=recv, device_id=where, device_id_type=MESH
    )


def global_body(
    bounds_ref, state_ref, weight_hbm, out_ref,
    weight, states, acc, kv_own, kv, queries, live, top, sums, mixed,
    w_sem, mp_send, mp_recv, q_send, q_recv, g_send, g_recv, up_send, up_recv, dn_send, dn_recv,
    o_send, o_recv,
):
    ctx = lax.axis_index("ctx")
    mp = lax.axis_index("mp")
    z = ctx // GROUP
    member = ctx % GROUP
    y = mp // 2
    xh = mp % 2

    def at_mp(yy, xx):
        return lax.rem(yy + 4, 4) * 2 + xx

    def mate(k):
        return z * GROUP + lax.rem(member + k, GROUP)

    y_up, y_dn, x_other = at_mp(y + 1, xh), at_mp(y - 1, xh), at_mp(y, 1 - xh)
    z_up = lax.rem(z + 1, N_Z) * GROUP + member
    z_dn = lax.rem(z + N_Z - 1, N_Z) * GROUP + member

    w_copy = pltpu.make_async_copy(weight_hbm, weight, w_sem)
    w_copy.start()

    barrier = pltpu.get_barrier_semaphore()
    partners = [{"ctx": ctx, "mp": y_up}, {"ctx": ctx, "mp": y_dn}, {"ctx": ctx, "mp": x_other},
                {"ctx": z_up, "mp": mp}, {"ctx": z_dn, "mp": mp}]
    partners += [{"ctx": mate(k), "mp": mp} for k in range(1, GROUP)]
    for partner in partners:
        pl.semaphore_signal(barrier, inc=1, device_id=partner, device_id_type=MESH)
    pl.semaphore_wait(barrier, len(partners))

    half = PCAP // 2
    lower, upper = pl.ds(0, half), pl.ds(half, half)
    whole = pl.ds(0, PCAP)

    def hand(src, block, rows, slot, to):
        return remote(src, states.at[block, rows], mp_send.at[slot], mp_recv.at[slot], {"ctx": ctx, "mp": to})

    own_x = hand(state_ref, mp, whole, 0, x_other)
    own_up = hand(state_ref, mp, whole, 1, y_up)
    own_dn = hand(state_ref, mp, whole, 2, y_dn)
    own_x.start()
    own_up.start()
    own_dn.start()
    states[mp] = state_ref[...]

    q_copies = []
    for k in range(1, GROUP):
        head = lax.rem(member + k, GROUP)
        copy = remote(
            state_ref.at[:, pl.ds(pl.multiple_of(head * HD, HD), HD)],
            queries.at[pl.ds(pl.multiple_of(member * PCAP, PCAP), PCAP)],
            q_send.at[k - 1], q_recv.at[k - 1], {"ctx": mate(k), "mp": mp},
        )
        copy.start()
        q_copies.append(copy)
    queries[pl.ds(pl.multiple_of(member * PCAP, PCAP), PCAP), :] = state_ref[
        :, pl.ds(pl.multiple_of(member * HD, HD), HD)
    ]

    w_copy.wait()

    def project(block, first=False):
        left = states[block]
        for n in range(4):
            rows = pl.ds(pl.multiple_of(block * COLS, COLS), COLS)
            right = weight[rows, :, n * HD : (n + 1) * HD]
            part = jnp.dot(left, right.reshape(COLS, 2 * HD), preferred_element_type=F32)
            cols = slice(n * 2 * HD, (n + 1) * 2 * HD)
            if first:
                acc[:, cols] = part
            else:
                acc[:, cols] += part

    project(mp, True)

    def arrived(block, rows, slot):
        hand(states.at[block, rows], block, rows, slot, y_up).wait_recv()

    far = at_mp(y + 2, xh)
    arrived(y_dn, whole, 1)
    fwd_up = hand(states.at[y_dn, lower], y_dn, lower, 3, y_up)
    fwd_up.start()
    arrived(y_up, whole, 2)
    fwd_dn = hand(states.at[y_up, upper], y_up, upper, 4, y_dn)
    fwd_dn.start()
    arrived(x_other, whole, 0)
    ox_up = hand(states.at[x_other], x_other, whole, 5, y_up)
    ox_dn = hand(states.at[x_other], x_other, whole, 6, y_dn)
    ox_up.start()
    ox_dn.start()
    project(y_dn)
    project(y_up)
    project(x_other)
    arrived(far, lower, 3)
    arrived(far, upper, 4)
    project(far)
    o_dn, o_up, o_far = at_mp(y - 1, 1 - xh), at_mp(y + 1, 1 - xh), at_mp(y + 2, 1 - xh)
    arrived(o_dn, whole, 5)
    ofwd_up = hand(states.at[o_dn, lower], o_dn, lower, 7, y_up)
    ofwd_up.start()
    arrived(o_up, whole, 6)
    ofwd_dn = hand(states.at[o_up, upper], o_up, upper, 8, y_dn)
    ofwd_dn.start()
    project(o_dn)
    project(o_up)
    arrived(o_far, lower, 7)
    arrived(o_far, upper, 8)
    project(o_far)

    mine = pl.ds(pl.multiple_of(member * PCAP, PCAP), PCAP)
    for n in range(HERE):
        for part in range(2):
            begin = n * 2 * HD + part * HD
            kv_own[part, n] = acc[:, begin : begin + HD].astype(BF16)
    g_copies = []
    for part in range(2):
        for k in range(1, GROUP):
            head = lax.rem(member + k, GROUP)
            slot = part * 3 + k - 1
            copy = remote(
                kv_own.at[part, head], kv.at[z, part, mine], g_send.at[slot], g_recv.at[slot],
                {"ctx": mate(k), "mp": mp},
            )
            copy.start()
            g_copies.append(copy)
        kv[z, part, mine, :] = kv_own[part, member]

    def ring(block, part, slot, up):
        block = lax.rem(block + N_Z, N_Z)
        send, recv, to = (up_send, up_recv, z_up) if up else (dn_send, dn_recv, z_dn)
        return remote(
            kv.at[block, part], kv.at[block, part], send.at[slot], recv.at[slot], {"ctx": to, "mp": mp}
        )

    ring_copies = []

    def send(block, part, slot, up):
        copy = ring(block, part, slot, up)
        copy.start()
        ring_copies.append(copy)

    for part in range(2):
        for k in range(3):
            g_copies[part * 3 + k].wait_recv()
        send(z, part, part, True)
        send(z, part, part, False)

    for copy in q_copies:
        copy.wait_recv()

    bounds = bounds_ref[...]
    alive = bounds[:, 1 : PCAP + 1] > bounds[:, :PCAP]
    live[...] = jnp.where(alive, 0.0, MASKED)

    def bias_of(block):
        rows = [live[pl.ds(block * GROUP + i, 1), :] for i in range(GROUP)]
        return jnp.concatenate(rows, axis=1)

    STEP = PCAP

    def attend(block, start):
        bias = bias_of(block)
        keys = kv[block, 0]
        values = kv[block, 1]

        def chunk(i, _):
            rows = pl.ds(pl.multiple_of(i * STEP, STEP), STEP)
            query = queries[rows, :]
            scores = lax.dot_general(
                query, keys, (((1,), (1,)), ((), ())), preferred_element_type=F32
            ) * SCALE + bias
            if start:
                key_at = lax.broadcasted_iota(jnp.int32, (STEP, ROWS), 1)
                query_at = lax.broadcasted_iota(jnp.int32, (STEP, ROWS), 0) + i * STEP
                scores = jnp.where(key_at <= query_at, scores, MASKED)
            best = jnp.max(scores, axis=1, keepdims=True)
            if not start:
                before = top[rows, :]
                best = jnp.maximum(best, before)
                keep = jnp.exp(before - best)
            weights = jnp.exp(scores - best)
            total = jnp.sum(weights, axis=1, keepdims=True)
            part = jnp.dot(weights.astype(BF16), values, preferred_element_type=F32)
            if start:
                sums[rows, :] = total
                mixed[rows, :] = part
            else:
                sums[rows, :] = sums[rows, :] * keep + total
                mixed[rows, :] = mixed[rows, :] * keep + part
            top[rows, :] = best
            return 0

        lax.fori_loop(0, ROWS // STEP, chunk, 0)

    attend(z, True)

    for hop in range(1, 5):
        for part in range(2):
            for up in (True, False):
                block = z - hop if up else z + hop
                if hop == 4 and part == (1 if up else 0):
                    continue
                slot = 2 * (hop - 1) + part if hop < 4 else 6
                ring(block, part, slot, up).wait_recv()
                if hop < 3:
                    send(block, part, 2 * hop + part, up)
                elif hop == 3 and part == (0 if up else 1):
                    send(block, part, 6, up)
        blocks = (z - hop, z + hop) if hop < 4 else (z - hop,)
        for block in blocks:
            index = lax.rem(block + N_Z, N_Z)

            @pl.when(index < z)
            def _():
                attend(index, False)

    bounds_z = [live[pl.ds(z * GROUP + i, 1), :] for i in range(GROUP)]
    eye = lax.broadcasted_iota(jnp.int32, (PCAP, PCAP), 0) == lax.broadcasted_iota(
        jnp.int32, (PCAP, PCAP), 1
    )
    for copy in g_copies:
        copy.wait_send()
    o_copies = []
    for i in range(GROUP):
        rows = pl.ds(i * PCAP, PCAP)
        dead = jnp.sum(jnp.where(eye, bounds_z[i], 0.0), axis=1, keepdims=True)
        value = jnp.where(dead < 0, 0.0, mixed[rows, :] / sums[rows, :])
        value = queries[rows, :].astype(F32) + value
        kv_own[0, i] = value.astype(BF16)
    column = pl.ds(pl.multiple_of(member * HD, HD), HD)
    for k in range(1, GROUP):
        index = lax.rem(member + k, GROUP)
        copy = remote(
            kv_own.at[0, index], out_ref.at[:, column], o_send.at[k - 1], o_recv.at[k - 1],
            {"ctx": mate(k), "mp": mp},
        )
        copy.start()
        o_copies.append(copy)
    out_ref[:, column] = kv_own[0, member]
    for copy in o_copies:
        copy.wait_recv()
    for copy in o_copies + q_copies + ring_copies + [own_x, own_up, own_dn, fwd_up, fwd_dn, ox_up, ox_dn, ofwd_up, ofwd_dn]:
        copy.wait_send()


def globally(bounds, state, weight):
    vmem = pl.BlockSpec(memory_space=pltpu.VMEM)
    dma = pltpu.SemaphoreType.DMA
    return pl.pallas_call(
        global_body,
        out_shape=jax.ShapeDtypeStruct((PCAP, COLS), BF16),
        in_specs=[vmem, vmem, pl.BlockSpec(memory_space=pl.ANY)],
        out_specs=vmem,
        scratch_shapes=[
            pltpu.VMEM((D, 2, COLS), BF16),
            pltpu.VMEM((N_MP, PCAP, COLS), BF16),
            pltpu.VMEM((PCAP, 2 * COLS), F32),
            pltpu.VMEM((2, HERE, PCAP, HD), BF16),
            pltpu.VMEM((N_Z, 2, ROWS, HD), BF16),
            pltpu.VMEM((ROWS, HD), BF16),
            pltpu.VMEM((32, PCAP), F32),
            pltpu.VMEM((ROWS, 1), F32),
            pltpu.VMEM((ROWS, 1), F32),
            pltpu.VMEM((ROWS, HD), F32),
            dma, dma((9,)), dma((9,)), dma((3,)), dma((3,)), dma((6,)), dma((6,)),
            dma((7,)), dma((7,)), dma((7,)), dma((7,)), dma((3,)), dma((3,)),
        ],
        compiler_params=pltpu.CompilerParams(
            vmem_limit_bytes=48 * 2**20, collective_id=0, has_side_effects=True
        ),
        name="globally",
    )(bounds, state, weight)


def shards(byte_qkv, kv_weight, patch_bounds):
    bytes3 = byte_qkv.transpose(1, 0, 2)
    count = lax.axis_size("ctx")
    edge = lax.ppermute(bytes3[:, :WIN], "ctx", [(i, i - 1) for i in range(1, count)])
    state = cross(patch_bounds, bytes3, edge)
    return globally(patch_bounds, state, kv_weight)


def solution(mesh):
    return jax.shard_map(
        shards,
        mesh=mesh,
        in_specs=(P("ctx", None, "mp"), P(None, None, "mp"), P()),
        out_specs=P("ctx", "mp"),
        check_vma=False,
    )
```

time: 253 us -> 75.2 us (0.30)
  waiting for transfers between devices: 118 us -> 1.15 us
  Pallas kernels: 0 us -> 64.2 us
  local copies, waits for them, and re-layouts: 64.2 us -> 4.39 us
  matrix products: 31.2 us -> 0 us
  other arithmetic: 20.3 us -> 0 us
  between operations: 13.6 us -> 0.04 us
    all_gather x2 -> x0, waiting for transfers between devices: 118 us -> none  [the longest x1 73 us: shards(): shard_piece = lax.all_gather(key_value, 'ctx', axis=0, tiled=True)]
    pallas_call x0 -> x2, Pallas kernels: none -> 64.2 us  [the longest x1 60.3 us: globally(): pl.pallas_call(global_body, out_shape=jax.ShapeDtypeStruct((PCAP, COLS),...]
    dot_general x5 -> x0, matrix products: 31.2 us -> none  [the longest x1 12.6 us: shards(): jnp.einsum('hqk,khd->hqd', exp_part, value_part.astype(jnp.float32), prec...]
    reshape x1 -> x0, local copies, waits for them, and re-layouts: 21.7 us -> none  [shards(): window = window.reshape(slot_count, WIN, 3, heads_here, head_dim)]
    unnamed x8 -> x7, local copies, waits for them, and re-layouts: 23.8 us -> 3.59 us
    gather x1 -> x0, local copies, waits for them, and re-layouts: 12.8 us -> none  [shards(): window = extended[local_start[:, None] + offsets[None, :]]]
    reduce_sum x1 -> x0, other arithmetic: 8.85 us -> none  [shards(): denom_sum = jnp.sum(exp_part, axis=2)]
    reduce_max x1 -> x0, other arithmetic: 5.35 us -> none  [shards(): jnp.max(jnp.where(inside[:, :, None, None], window[:, :, 0], -jnp.inf), a...]
  transfers between devices with their start and end apart: 3 -> 1, of which waited for: 3 -> 1; matrix products, arithmetic and copies ran while one was open for 4% -> 0% of each run, Pallas kernels for 0% -> 0%
where the time goes in v1:
time: 75.2 us; the launch traced here: 74.9 us
  Pallas kernels  64.2 us (85%)
  starting transfers between devices  5.1 us (7%)
  local copies, waits for them, and re-layouts  4.39 us (6%)
  waiting for transfers between devices  1.15 us (2%)
    pallas_call x1, Pallas kernels, globally(): pl.pallas_call(global_body, out_shape=jax.ShapeDtypeStruct((PCAP, COLS),...  60.3 us
    ppermute x1, starting transfers between devices, shards(): lax.ppermute(bytes3[:, :WIN], 'ctx', [(i, i - 1) for i in range(1, count)])  5.1 us
    pallas_call x1, Pallas kernels, cross(): pl.pallas_call(cross_body, out_shape=jax.ShapeDtypeStruct((PCAP, COLS), B...  3.92 us
    unnamed x7, local copies, waits for them, and re-layouts  3.59 us
  transfers between devices with their start and end apart: 1, of which 1 were waited for; matrix products, arithmetic and copies ran while one was open for 0% of the time, Pallas kernels for 0%

profile of v1, /device:TPU:1, one launch (start us, length us, event | category | flops | bytes accessed | tf_op | source)
XLA Modules:
  0.0 74.9 jit_solution(17380459610881538854)
XLA Ops:
  0.0 0.8 %slice.4 = bf16[3,16,512]{2,1,0:T(8,128)(2,1)S(1)} slice(bf16[3,512,512]{2,1,0:T(8,128)(2,1)} %bitcast.1), slice={[0:3], [0:16], [0:512]} | slice | bytes 98304 | tf_op jit(solution)/shard_map/slice | solution.py:371
  0.8 5.1 %collective-permute-start = (bf16[3,16,512]{2,1,0:T(8,128)(2,1)S(1)}, bf16[3,16,512]{2,1,0:T(8,128)(2,1)S(1)}, u32[]{:S(2)}, u32[]{:S(2)}) collective-permute-start(bf16[3,16,512]{2,1,0:T(8,128)(2,1)S(1)} %slice.4), channel_id=1, source_target_pairs={{8,0},{16,8},{24,16},{32,24},{40,32},{48,40},{56,48},{64,56},{72,6... | collective-permute-start | bytes 147464 | tf_op jit(solution)/shard_map/ppermute | solution.py:371
  5.9 1.1 %collective-permute-done.edge_ref = bf16[3,16,512]{2,1,0:T(8,128)(2,1)S(1)} collective-permute-done((bf16[3,16,512]{2,1,0:T(8,128)(2,1)S(1)}, bf16[3,16,512]{2,1,0:T(8,128)(2,1)S(1)}, u32[]{:S(2)}, u32[]{:S(2)}) %collective-permute-start) | collective-permute-done | bytes 49184 | tf_op jit(solution)/shard_map/ppermute | solution.py:371
  7.1 0.0 copy-start
  7.1 1.4 %copy-done = bf16[512,3,512]{2,0,1:T(8,128)(2,1)S(1)} copy-done((bf16[512,3,512]{2,0,1:T(8,128)(2,1)S(1)}, bf16[512,3,512]{2,0,1:T(8,128)(2,1)}, u32[]{:S(2)}) %copy-start) | copy-done | bytes 1572888
  8.5 0.0 copy-start.1
  8.5 0.8 %copy-done.1 = s32[32,161]{1,0:T(8,128)S(1)} copy-done((s32[32,161]{1,0:T(8,128)S(1)}, s32[32,161]{1,0:T(8,128)}, u32[]{:S(2)}) %copy-start.1) | copy-done | bytes 20632
  9.2 3.9 %cross.1.state_ref = bf16[160,512]{1,0:T(8,128)(2,1)S(1)} custom-call(s32[32,161]{1,0:T(8,128)S(1)} %copy-done.1, bf16[3,512,512]{2,1,0:T(8,128)(2,1)S(1)} %bitcast.2, bf16[3,16,512]{2,1,0:T(8,128)(2,1)S(1)} %collective-permute-done.edge_ref), custom_call_target="tpu_custom_call" | custom-call | tf_op jit(solution)/shard_map/cross/pallas_call | solution.py:73
  13.1 0.0 copy-start.2
  13.2 0.7 %copy-done.2 = s32[32,161]{1,0:T(8,128)S(1)} copy-done((s32[32,161]{1,0:T(8,128)S(1)}, s32[32,161]{1,0:T(8,128)}, u32[]{:S(2)}) %copy-start.2) | copy-done | bytes 20632
  13.9 60.3 %globally.1 = bf16[160,512]{1,0:T(8,128)(2,1)S(1)} custom-call(s32[32,161]{1,0:T(8,128)S(1)} %copy-done.2, bf16[160,512]{1,0:T(8,128)(2,1)S(1)} %cross.1.state_ref, bf16[4096,2,512]{2,1,0:T(2,128)(2,1)} %weight_hbm.1), custom_call_target="tpu_custom_call" | custom-call | tf_op jit(solution)/shard_map/globally/pallas_call | solution.py:342
  74.2 0.7 copy.5
Async XLA Ops:
  0.8 6.3 %collective-permute-start = (bf16[3,16,512]{2,1,0:T(8,128)(2,1)S(1)}, bf16[3,16,512]{2,1,0:T(8,128)(2,1)S(1)}, u32[]{:S(2)}, u32[]{:S(2)}) collective-permute-start(bf16[3,16,512]{2,1,0:T(8,128)(2,1)S(1)} %slice.4), channel_id=1, source_target_pairs={{8,0},{16,8},{24,16},{32,24},{40,32},{48,40},{56,48},{64,56},{72,6... | collective-permute-start | bytes 147464 | tf_op jit(solution)/shard_map/ppermute | solution.py:371
  7.1 1.4 %copy-start = (bf16[512,3,512]{2,0,1:T(8,128)(2,1)S(1)}, bf16[512,3,512]{2,0,1:T(8,128)(2,1)}, u32[]{:S(2)}) copy-start(bf16[512,3,512]{2,0,1:T(8,128)(2,1)} %param.3) | copy-start | bytes 4718596
  8.5 0.8 %copy-start.1 = (s32[32,161]{1,0:T(8,128)S(1)}, s32[32,161]{1,0:T(8,128)}, u32[]{:S(2)}) copy-start(s32[32,161]{1,0:T(8,128)} %bounds_ref.3) | copy-start | bytes 61828
  13.1 0.8 %copy-start.2 = (s32[32,161]{1,0:T(8,128)S(1)}, s32[32,161]{1,0:T(8,128)}, u32[]{:S(2)}) copy-start(s32[32,161]{1,0:T(8,128)} %bounds_ref.3) | copy-start | bytes 61828

commit v2 on v0

v2 whole, which is shorter than its diff:
```python
import math

import jax
import jax.numpy as jnp
from jax import lax
from jax.experimental import pallas as pl
from jax.experimental.pallas import tpu as pltpu
from jax.sharding import PartitionSpec as P

D = 4096
HEADS = 32
WIN = 16
HD = 128
BYTE_DEV = 512
EXT = BYTE_DEV + WIN
PCAP = 160
COLS = 512
HERE = 4
N_MP = 8
N_Z = 8
GROUP = 4
ROWS = GROUP * PCAP
SCALE = 1.0 / math.sqrt(HD)
SCALE2 = SCALE * math.log2(math.e)
EDGE = BYTE_DEV - 2 * WIN
MASKED = -1e30
F32 = jnp.float32
BF16 = jnp.bfloat16
CHUNKS = ((0, 64), (64, 96))
MESH = pl.DeviceIdType.MESH


def remote(src, dst, send, recv, where):
    return pltpu.make_async_remote_copy(
        src_ref=src, dst_ref=dst, send_sem=send, recv_sem=recv, device_id=where, device_id_type=MESH
    )


def kernel(
    bounds_hbm, bytes_hbm, weight_hbm, out_ref,
    bounds_ref, ext, tops, state, weight, plain, states, acc, own0, own1, kv0, kv1,
    queries, live, bias0, bias1, top, mixed, outgoing,
    in_sem, halo_send, halo_recv, mp_send, mp_recv, q_send, q_recv, g_send, g_recv,
    up_send, up_recv, dn_send, dn_recv, o_send, o_recv,
):
    ctx = lax.axis_index("ctx")
    mp = lax.axis_index("mp")
    z = ctx // GROUP
    member = ctx % GROUP
    y = mp // 2
    xh = mp % 2
    owns, kvs, biases = (own0, own1), (kv0, kv1), (bias0, bias1)
    sent = []

    def at_mp(yy, xx):
        return lax.rem(yy + 4, 4) * 2 + xx

    def mate(k):
        return z * GROUP + lax.rem(member + k, GROUP)

    y_up, y_dn, x_other = at_mp(y + 1, xh), at_mp(y - 1, xh), at_mp(y, 1 - xh)
    far = at_mp(y + 2, xh)
    o_dn, o_up, o_far = at_mp(y - 1, 1 - xh), at_mp(y + 1, 1 - xh), at_mp(y + 2, 1 - xh)
    z_up = lax.rem(z + 1, N_Z) * GROUP + member
    z_dn = lax.rem(z + N_Z - 1, N_Z) * GROUP + member
    before_me = lax.rem(ctx + N_Z * GROUP - 1, N_Z * GROUP)
    after_me = lax.rem(ctx + 1, N_Z * GROUP)

    bounds_in = pltpu.make_async_copy(bounds_hbm, bounds_ref, in_sem.at[0])
    bytes_in = pltpu.make_async_copy(bytes_hbm, ext.at[:, pl.ds(0, BYTE_DEV)], in_sem.at[1])
    weight_in = pltpu.make_async_copy(weight_hbm, weight, in_sem.at[2])
    bounds_in.start()
    bytes_in.start()
    weight_in.start()

    barrier = pltpu.get_barrier_semaphore()
    partners = [{"ctx": before_me, "mp": mp}, {"ctx": after_me, "mp": mp},
                {"ctx": ctx, "mp": y_up}, {"ctx": ctx, "mp": y_dn}, {"ctx": ctx, "mp": x_other},
                {"ctx": z_up, "mp": mp}, {"ctx": z_dn, "mp": mp}]
    partners += [{"ctx": mate(k), "mp": mp} for k in range(1, GROUP)]
    for partner in partners:
        pl.semaphore_signal(barrier, inc=1, device_id=partner, device_id_type=MESH)
    pl.semaphore_wait(barrier, len(partners))

    halo = remote(
        bytes_hbm.at[:, pl.ds(0, WIN)], ext.at[:, pl.ds(BYTE_DEV, WIN)], halo_send, halo_recv,
        {"ctx": before_me, "mp": mp},
    )
    halo.start()
    sent.append(halo)

    bounds_in.wait()
    row = bounds_ref[pl.ds(ctx, 1), :] - ctx * BYTE_DEV
    starts = row[:, :PCAP]
    ends = row[:, 1 : PCAP + 1]
    diag = lax.broadcasted_iota(jnp.int32, (PCAP, PCAP), 0) == lax.broadcasted_iota(
        jnp.int32, (PCAP, PCAP), 1
    )
    start_col = jnp.sum(jnp.where(diag, starts, 0), axis=1, keepdims=True)
    end_col = jnp.sum(jnp.where(diag, ends, 0), axis=1, keepdims=True)
    byte_col = lax.broadcasted_iota(jnp.int32, (EXT, PCAP), 0)
    inside_t = (byte_col >= starts) & (byte_col < ends)
    left = jnp.sum(jnp.where(inside_t, ends - byte_col, 0), axis=1, keepdims=True)

    def patch_tops(begin, end):
        room = left[begin:end]
        for h in range(HERE):
            cols = slice(h * HD, (h + 1) * HD)
            best = ext[0, begin:end, cols].astype(F32)
            for shift in (1, 2, 4, 8):
                later = pltpu.roll(best, end - begin - shift, 0)
                best = jnp.maximum(best, jnp.where(room > shift, later, -jnp.inf))
            tops[begin:end, cols] = best.astype(BF16)

    bytes_in.wait()
    patch_tops(0, BYTE_DEV)
    halo.wait_recv()
    patch_tops(EDGE, EXT)

    def cross(off, count):
        begin, end = start_col[off : off + count], end_col[off : off + count]
        byte_row = lax.broadcasted_iota(jnp.int32, (count, EXT), 1)
        inside = (byte_row >= begin) & (byte_row < end)
        first = ((byte_row == begin) & (end > begin)).astype(F32).astype(BF16)
        for h in range(HERE):
            cols = slice(h * HD, (h + 1) * HD)
            query = jnp.dot(first, tops[:, cols], preferred_element_type=F32).astype(BF16)
            scores = (
                lax.dot_general(
                    query, ext[1, :, cols], (((1,), (1,)), ((), ())), preferred_element_type=F32
                )
                * SCALE
            )
            scores = jnp.where(inside, scores, MASKED)
            scores = scores - jnp.max(scores, axis=1, keepdims=True)
            terms = jnp.where(inside, jnp.exp(scores), 0.0)
            total = jnp.sum(terms, axis=1, keepdims=True)
            weights = (terms / jnp.where(total > 0, total, 1.0)).astype(BF16)
            state[off : off + count, cols] = jnp.dot(
                weights, ext[2, :, cols], preferred_element_type=F32
            ).astype(BF16)

    def rows_of(c, part=None):
        off, count = CHUNKS[c]
        if part is None:
            return pl.ds(off, count)
        return pl.ds(off + part * (count // 2), count // 2)

    def hand(c, src, block, rows, slot, to):
        slot = 9 * c + slot
        return remote(src, states.at[block, rows], mp_send.at[slot], mp_recv.at[slot], {"ctx": ctx, "mp": to})

    def pass_on(c, block, part, slot, to, own=False):
        rows = rows_of(c, part)
        src = state.at[rows] if own else states.at[block, rows]
        copy = hand(c, src, block, rows, slot, to)
        copy.start()
        sent.append(copy)

    def arrived(c, block, part, slot):
        rows = rows_of(c, part)
        hand(c, states.at[block, rows], block, rows, slot, y_up).wait_recv()

    def send_own(c):
        pass_on(c, mp, None, 0, x_other, True)
        pass_on(c, mp, None, 1, y_up, True)
        pass_on(c, mp, None, 2, y_dn, True)

    def near(c):
        arrived(c, y_dn, None, 1)
        pass_on(c, y_dn, 0, 3, y_up)
        arrived(c, y_up, None, 2)
        pass_on(c, y_up, 1, 4, y_dn)

    def across(c):
        arrived(c, x_other, None, 0)
        pass_on(c, x_other, None, 5, y_up)
        pass_on(c, x_other, None, 6, y_dn)

    def across_near(c):
        arrived(c, o_dn, None, 5)
        pass_on(c, o_dn, 0, 7, y_up)
        arrived(c, o_up, None, 6)
        pass_on(c, o_up, 1, 8, y_dn)

    def prepare(block):
        rows = pl.ds(pl.multiple_of(block * COLS, COLS), COLS)
        plain[block] = weight[rows].reshape(COLS, 2 * COLS)

    def project(c, block, first=False):
        rows = rows_of(c)
        part_rows = (state if first else states.at[block])[rows, :]
        part = jnp.dot(part_rows, plain[block], preferred_element_type=F32)
        if first:
            acc[rows, :] = part
        else:
            acc[rows, :] += part

    def exchange(c):
        off, count = CHUNKS[c]
        own, kv = owns[c], kvs[c]
        mine = pl.ds(pl.multiple_of(member * count, count), count)
        for part in range(2):
            for n in range(HERE):
                begin = part * COLS + n * HD
                own[part, n] = acc[off : off + count, begin : begin + HD].astype(BF16)
        copies = []
        for part in range(2):
            for k in range(1, GROUP):
                slot = 6 * c + part * 3 + k - 1
                copy = remote(
                    own.at[part, lax.rem(member + k, GROUP)], kv.at[z, part, mine],
                    g_send.at[slot], g_recv.at[slot], {"ctx": mate(k), "mp": mp},
                )
                copy.start()
                copies.append(copy)
                sent.append(copy)
            kv[z, part, mine, :] = own[part, member]
        return copies

    def piece(c, block, part, slot, up):
        block = lax.rem(block + N_Z, N_Z)
        slot = 7 * c + slot
        send, recv, to = (up_send, up_recv, z_up) if up else (dn_send, dn_recv, z_dn)
        ref = kvs[c].at[block, part]
        return remote(ref, ref, send.at[slot], recv.at[slot], {"ctx": to, "mp": mp})

    def ring_send(c, block, part, slot, up):
        copy = piece(c, block, part, slot, up)
        copy.start()
        sent.append(copy)

    def ring_start(c, copies):
        for part in range(2):
            for k in range(3):
                copies[part * 3 + k].wait_recv()
            ring_send(c, z, part, part, True)
            ring_send(c, z, part, part, False)

    def ring_hop(c, hop):
        for part in range(2):
            for up in (True, False):
                block = z - hop if up else z + hop
                if hop == 4 and part == (1 if up else 0):
                    continue
                slot = 2 * (hop - 1) + part if hop < 4 else 6
                piece(c, block, part, slot, up).wait_recv()
                if hop < 3:
                    ring_send(c, block, part, 2 * hop + part, up)
                elif hop == 3 and part == (0 if up else 1):
                    ring_send(c, block, part, 6, up)

    def attend(c, block, own):
        off, count = CHUNKS[c]
        keys_here = GROUP * count
        start = own and c == 0
        bias = biases[c][pl.ds(block, 1), :]
        keys = kvs[c][block, 0]
        values = jnp.concatenate([kvs[c][block, 1], jnp.ones((keys_here, HD), BF16)], axis=1)
        for i in range(GROUP):
            rows = slice(i * PCAP, (i + 1) * PCAP)
            scores = lax.dot_general(
                queries[rows, :], keys, (((1,), (1,)), ((), ())), preferred_element_type=F32
            ) + bias
            if own:
                at = lax.broadcasted_iota(jnp.int32, (1, keys_here), 1)
                slot = at + off
                for m in range(1, GROUP):
                    slot = slot + jnp.where(at >= m * count, PCAP - count, 0)
                query_at = lax.broadcasted_iota(jnp.int32, (PCAP, keys_here), 0) + i * PCAP
                scores = jnp.where(slot <= query_at, scores, MASKED)
            best = jnp.max(scores, axis=1, keepdims=True)
            if not start:
                before = top[rows, :]
                best = jnp.maximum(best, before)
                keep = jnp.exp2((before - best) * SCALE2)
            weights = jnp.exp2((scores - best) * SCALE2)
            part = jnp.dot(weights.astype(BF16), values, preferred_element_type=F32)
            if not start:
                part = mixed[rows, :] * keep + part
            mixed[rows, :] = part
            top[rows, :] = best

    def attend_hop(c, hop):
        def one(d, _):
            index = lax.rem(z + (2 * d - 1) * hop + N_Z, N_Z)

            @pl.when(index < z)
            def _():
                attend(c, index, False)

            return 0

        lax.fori_loop(0, 2 if hop < 4 else 1, one, 0)

    cross(*CHUNKS[0])
    send_own(0)
    cross(*CHUNKS[1])
    send_own(1)
    own_rows = pl.ds(pl.multiple_of(member * PCAP, PCAP), PCAP)
    q_copies = []
    for k in range(1, GROUP):
        head = lax.rem(member + k, GROUP)
        copy = remote(
            state.at[:, pl.ds(pl.multiple_of(head * HD, HD), HD)], queries.at[own_rows],
            q_send.at[k - 1], q_recv.at[k - 1], {"ctx": mate(k), "mp": mp},
        )
        copy.start()
        q_copies.append(copy)
        sent.append(copy)
    queries[own_rows, :] = state[:, pl.ds(pl.multiple_of(member * HD, HD), HD)]

    weight_in.wait()
    near(0)
    prepare(mp)
    project(0, mp, True)
    prepare(y_dn)
    project(0, y_dn)
    prepare(y_up)
    project(0, y_up)
    across(0)
    near(1)
    for block in (x_other, far, o_dn, o_up, o_far):
        prepare(block)
    project(0, x_other)
    arrived(0, far, 0, 3)
    arrived(0, far, 1, 4)
    project(0, far)
    across_near(0)
    project(0, o_dn)
    project(0, o_up)
    across(1)
    arrived(0, o_far, 0, 7)
    arrived(0, o_far, 1, 8)
    project(0, o_far)
    g0 = exchange(0)

    bounds = bounds_ref[...]
    live[...] = jnp.where(bounds[:, 1 : PCAP + 1] > bounds[:, :PCAP], 0.0, MASKED)
    for c, (off, count) in enumerate(CHUNKS):
        for block in range(N_Z):
            biases[c][block : block + 1, :] = jnp.concatenate(
                [live[block * GROUP + i : block * GROUP + i + 1, off : off + count] for i in range(GROUP)],
                axis=1,
            )
    project(1, mp, True)
    project(1, y_dn)
    ring_start(0, g0)
    project(1, y_up)
    arrived(1, far, 0, 3)
    arrived(1, far, 1, 4)
    project(1, far)
    project(1, x_other)
    for copy in q_copies:
        copy.wait_recv()
    attend(0, z, True)
    across_near(1)
    project(1, o_dn)
    project(1, o_up)
    ring_hop(0, 1)
    arrived(1, o_far, 0, 7)
    arrived(1, o_far, 1, 8)
    project(1, o_far)
    g1 = exchange(1)
    attend_hop(0, 1)
    ring_hop(0, 2)
    ring_start(1, g1)
    attend(1, z, True)
    attend_hop(0, 2)
    ring_hop(0, 3)
    attend_hop(0, 3)
    ring_hop(1, 1)
    ring_hop(0, 4)
    attend_hop(0, 4)
    attend_hop(1, 1)
    for hop in range(2, 5):
        ring_hop(1, hop)
        attend_hop(1, hop)

    column = pl.ds(pl.multiple_of(member * HD, HD), HD)
    o_copies = []
    for k in (2, 1, 3, 0):
        index = lax.rem(member + k, GROUP)
        rows = pl.ds(pl.multiple_of(index * PCAP, PCAP), PCAP)
        dead = jnp.sum(jnp.where(diag, live[pl.ds(z * GROUP + index, 1), :], 0.0), axis=1, keepdims=True)
        value = jnp.where(dead < 0, 0.0, mixed[rows, :HD] / mixed[rows, HD:])
        outgoing[k] = (queries[rows, :].astype(F32) + value).astype(BF16)
        if k:
            copy = remote(
                outgoing.at[k], out_ref.at[:, column], o_send.at[k - 1], o_recv.at[k - 1],
                {"ctx": mate(k), "mp": mp},
            )
            copy.start()
            o_copies.append(copy)
            sent.append(copy)
    out_ref[:, column] = outgoing[0]
    for copy in o_copies:
        copy.wait_recv()
    for copy in sent:
        copy.wait_send()


def shards(byte_qkv, kv_weight, patch_bounds):
    anywhere = pl.BlockSpec(memory_space=pltpu.HBM)
    dma = pltpu.SemaphoreType.DMA
    (_, n0), (_, n1) = CHUNKS
    return pl.pallas_call(
        kernel,
        out_shape=jax.ShapeDtypeStruct((PCAP, COLS), BF16),
        in_specs=[anywhere, anywhere, anywhere],
        out_specs=pl.BlockSpec(memory_space=pltpu.VMEM),
        scratch_shapes=[
            pltpu.VMEM((32, PCAP + 1), jnp.int32),
            pltpu.VMEM((3, EXT, COLS), BF16),
            pltpu.VMEM((EXT, COLS), BF16),
            pltpu.VMEM((PCAP, COLS), BF16),
            pltpu.VMEM((D, 2, COLS), BF16),
            pltpu.VMEM((N_MP, COLS, 2 * COLS), BF16),
            pltpu.VMEM((N_MP, PCAP, COLS), BF16),
            pltpu.VMEM((PCAP, 2 * COLS), F32),
            pltpu.VMEM((2, HERE, n0, HD), BF16),
            pltpu.VMEM((2, HERE, n1, HD), BF16),
            pltpu.VMEM((N_Z, 2, GROUP * n0, HD), BF16),
            pltpu.VMEM((N_Z, 2, GROUP * n1, HD), BF16),
            pltpu.VMEM((ROWS, HD), BF16),
            pltpu.VMEM((32, PCAP), F32),
            pltpu.VMEM((N_Z, GROUP * n0), F32),
            pltpu.VMEM((N_Z, GROUP * n1), F32),
            pltpu.VMEM((ROWS, 1), F32),
            pltpu.VMEM((ROWS, 2 * HD), F32),
            pltpu.VMEM((GROUP, PCAP, HD), BF16),
            dma((3,)), dma, dma, dma((18,)), dma((18,)), dma((3,)), dma((3,)), dma((12,)), dma((12,)),
            dma((14,)), dma((14,)), dma((14,)), dma((14,)), dma((3,)), dma((3,)),
        ],
        compiler_params=pltpu.CompilerParams(
            vmem_limit_bytes=60 * 2**20, collective_id=0, has_side_effects=True
        ),
        name="patches",
    )(patch_bounds, byte_qkv.transpose(1, 0, 2), kv_weight)


def solution(mesh):
    return jax.shard_map(
        shards,
        mesh=mesh,
        in_specs=(P("ctx", None, "mp"), P(None, None, "mp"), P()),
        out_specs=P("ctx", "mp"),
        check_vma=False,
    )
```

time: 253 us -> 67.9 us (0.27)
  waiting for transfers between devices: 118 us -> 0 us
  Pallas kernels: 0 us -> 66.2 us
  local copies, waits for them, and re-layouts: 64.2 us -> 1.59 us
  matrix products: 31.2 us -> 0 us
  other arithmetic: 20.3 us -> 0 us
  between operations: 13.6 us -> 0.01 us
  starting transfers between devices: 5.33 us -> 0 us
    all_gather x2 -> x0, waiting for transfers between devices: 118 us -> none  [the longest x1 73 us: shards(): shard_piece = lax.all_gather(key_value, 'ctx', axis=0, tiled=True)]
    pallas_call x0 -> x1, Pallas kernels: none -> 66.2 us  [shards(): pl.pallas_call(kernel, out_shape=jax.ShapeDtypeStruct((PCAP, COLS), BF16)...]
    dot_general x5 -> x0, matrix products: 31.2 us -> none  [the longest x1 12.6 us: shards(): jnp.einsum('hqk,khd->hqd', exp_part, value_part.astype(jnp.float32), prec...]
    unnamed x8 -> x1, local copies, waits for them, and re-layouts: 23.8 us -> 1.59 us
    reshape x1 -> x0, local copies, waits for them, and re-layouts: 21.7 us -> none  [shards(): window = window.reshape(slot_count, WIN, 3, heads_here, head_dim)]
    gather x1 -> x0, local copies, waits for them, and re-layouts: 12.8 us -> none  [shards(): window = extended[local_start[:, None] + offsets[None, :]]]
    reduce_sum x1 -> x0, other arithmetic: 8.85 us -> none  [shards(): denom_sum = jnp.sum(exp_part, axis=2)]
    reduce_max x1 -> x0, other arithmetic: 5.35 us -> none  [shards(): jnp.max(jnp.where(inside[:, :, None, None], window[:, :, 0], -jnp.inf), a...]
  transfers between devices with their start and end apart: 3 -> 0, of which waited for: 3 -> 0; matrix products, arithmetic and copies ran while one was open for 4% -> 0% of each run, Pallas kernels for 0% -> 0%
where the time goes in v2:
time: 67.9 us; the launch traced here: 67.8 us
  Pallas kernels  66.2 us (97%)
  local copies, waits for them, and re-layouts  1.59 us (2%)
    pallas_call x1, Pallas kernels, shards(): pl.pallas_call(kernel, out_shape=jax.ShapeDtypeStruct((PCAP, COLS), BF16)...  66.2 us
    unnamed x1, local copies, waits for them, and re-layouts  1.59 us

profile of v2, /device:TPU:1, one launch (start us, length us, event | category | flops | bytes accessed | tf_op | source)
XLA Modules:
  0.0 67.8 jit_solution(16741749202784664140)
XLA Ops:
  0.0 66.2 %patches.1 = bf16[160,512]{1,0:T(8,128)(2,1)} custom-call(s32[32,161]{1,0:T(8,128)} %bounds_hbm.1, bf16[3,512,512]{2,1,0:T(8,128)(2,1)} %bitcast.1, bf16[4096,2,512]{2,1,0:T(2,128)(2,1)} %weight_hbm.1), custom_call_target="tpu_custom_call" | custom-call | tf_op jit(solution)/shard_map/patches/pallas_call | solution.py:407
  66.2 1.6 %copy.5 = bf16[160,512]{1,0:T(8,128)(2,1)} copy(bf16[160,512]{1,0:T(8,128)(2,1)} %patches.1) | data formatting | bytes 327680

commit v3 on v2

--- a/solution.py
+++ b/solution.py
@@ -38,7 +38,7 @@
 
 def kernel(
     bounds_hbm, bytes_hbm, weight_hbm, out_ref,
-    bounds_ref, ext, tops, state, weight, plain, states, acc, own0, own1, kv0, kv1,
+    bounds_ref, ext, tops, state, weight, plain, states, relay, acc, own0, own1, kv0, kv1,
     queries, live, bias0, bias1, top, mixed, outgoing,
     in_sem, halo_send, halo_recv, mp_send, mp_recv, q_send, q_recv, g_send, g_recv,
     up_send, up_recv, dn_send, dn_recv, o_send, o_recv,
@@ -75,7 +75,7 @@
 
     barrier = pltpu.get_barrier_semaphore()
     partners = [{"ctx": before_me, "mp": mp}, {"ctx": after_me, "mp": mp},
-                {"ctx": ctx, "mp": y_up}, {"ctx": ctx, "mp": y_dn}, {"ctx": ctx, "mp": x_other},
+                {"ctx": ctx, "mp": y_up}, {"ctx": ctx, "mp": y_dn}, {"ctx": mate(2), "mp": x_other},
                 {"ctx": z_up, "mp": mp}, {"ctx": z_dn, "mp": mp}]
     partners += [{"ctx": mate(k), "mp": mp} for k in range(1, GROUP)]
     for partner in partners:
@@ -147,7 +147,7 @@
         return pl.ds(off + part * (count // 2), count // 2)
 
     def hand(c, src, block, rows, slot, to):
-        slot = 9 * c + slot
+        slot = 12 * c + slot
         return remote(src, states.at[block, rows], mp_send.at[slot], mp_recv.at[slot], {"ctx": ctx, "mp": to})
 
     def pass_on(c, block, part, slot, to, own=False):
@@ -161,8 +161,25 @@
         rows = rows_of(c, part)
         hand(c, states.at[block, rows], block, rows, slot, y_up).wait_recv()
 
+    def x_hop(c, src, dst, slot, to):
+        slot = 12 * c + slot
+        return remote(src, dst, mp_send.at[slot], mp_recv.at[slot], {"ctx": mate(2), "mp": to})
+
+    def hop(c, src, dst, slot, to):
+        copy = x_hop(c, src, dst, slot, to)
+        copy.start()
+        sent.append(copy)
+
+    def relay_on(c):
+        for part, block, to in ((0, mp, x_other), (1, x_other, mp)):
+            rows = rows_of(c, part)
+            x_hop(c, relay.at[rows], relay.at[rows], 10 + part, to).wait_recv()
+            hop(c, relay.at[rows], states.at[block, rows], 9 * part, to)
+
     def send_own(c):
-        pass_on(c, mp, None, 0, x_other, True)
+        for part, to in ((0, mp), (1, x_other)):
+            rows = rows_of(c, part)
+            hop(c, state.at[rows], relay.at[rows], 10 + part, to)
         pass_on(c, mp, None, 1, y_up, True)
         pass_on(c, mp, None, 2, y_dn, True)
 
@@ -173,7 +190,8 @@
         pass_on(c, y_up, 1, 4, y_dn)
 
     def across(c):
-        arrived(c, x_other, None, 0)
+        arrived(c, x_other, 0, 0)
+        arrived(c, x_other, 1, 9)
         pass_on(c, x_other, None, 5, y_up)
         pass_on(c, x_other, None, 6, y_dn)
 
@@ -250,15 +268,15 @@
                 elif hop == 3 and part == (0 if up else 1):
                     ring_send(c, block, part, 6, up)
 
-    def attend(c, block, own):
+    def attend(c, block, own, chunks=range(GROUP)):
         off, count = CHUNKS[c]
         keys_here = GROUP * count
         start = own and c == 0
         bias = biases[c][pl.ds(block, 1), :]
         keys = kvs[c][block, 0]
         values = jnp.concatenate([kvs[c][block, 1], jnp.ones((keys_here, HD), BF16)], axis=1)
-        for i in range(GROUP):
-            rows = slice(i * PCAP, (i + 1) * PCAP)
+        for i in chunks:
+            rows = pl.ds(i * PCAP if isinstance(i, int) else pl.multiple_of(i * PCAP, PCAP), PCAP)
             scores = lax.dot_general(
                 queries[rows, :], keys, (((1,), (1,)), ((), ())), preferred_element_type=F32
             ) + bias
@@ -296,7 +314,16 @@
     cross(*CHUNKS[0])
     send_own(0)
     cross(*CHUNKS[1])
+    relay_on(0)
     send_own(1)
+    weight_in.wait()
+    near(0)
+    prepare(mp)
+    project(0, mp, True)
+    prepare(y_dn)
+    project(0, y_dn)
+    across(0)
+    relay_on(1)
     own_rows = pl.ds(pl.multiple_of(member * PCAP, PCAP), PCAP)
     q_copies = []
     for k in range(1, GROUP):
@@ -309,31 +336,32 @@
         q_copies.append(copy)
         sent.append(copy)
     queries[own_rows, :] = state[:, pl.ds(pl.multiple_of(member * HD, HD), HD)]
-
-    weight_in.wait()
-    near(0)
-    prepare(mp)
-    project(0, mp, True)
-    prepare(y_dn)
-    project(0, y_dn)
     prepare(y_up)
     project(0, y_up)
-    across(0)
+    prepare(x_other)
+    project(0, x_other)
     near(1)
-    for block in (x_other, far, o_dn, o_up, o_far):
+    for block in (far, o_dn, o_up, o_far):
         prepare(block)
-    project(0, x_other)
     arrived(0, far, 0, 3)
     arrived(0, far, 1, 4)
     project(0, far)
     across_near(0)
+    across(1)
     project(0, o_dn)
     project(0, o_up)
-    across(1)
     arrived(0, o_far, 0, 7)
     arrived(0, o_far, 1, 8)
     project(0, o_far)
     g0 = exchange(0)
+    for n, block in enumerate((mp, y_dn, y_up, x_other)):
+        project(1, block, n == 0)
+    across_near(1)
+    arrived(1, far, 0, 3)
+    arrived(1, far, 1, 4)
+    for block in (far, o_dn, o_up):
+        project(1, block)
+    ring_start(0, g0)
 
     bounds = bounds_ref[...]
     live[...] = jnp.where(bounds[:, 1 : PCAP + 1] > bounds[:, :PCAP], 0.0, MASKED)
@@ -343,45 +371,35 @@
                 [live[block * GROUP + i : block * GROUP + i + 1, off : off + count] for i in range(GROUP)],
                 axis=1,
             )
-    project(1, mp, True)
-    project(1, y_dn)
-    ring_start(0, g0)
-    project(1, y_up)
-    arrived(1, far, 0, 3)
-    arrived(1, far, 1, 4)
-    project(1, far)
-    project(1, x_other)
-    for copy in q_copies:
-        copy.wait_recv()
-    attend(0, z, True)
-    across_near(1)
-    project(1, o_dn)
-    project(1, o_up)
-    ring_hop(0, 1)
     arrived(1, o_far, 0, 7)
     arrived(1, o_far, 1, 8)
     project(1, o_far)
     g1 = exchange(1)
+    ring_hop(0, 1)
+    for copy in q_copies:
+        copy.wait_recv()
+    attend(0, z, True)
+    ring_start(1, g1)
+    attend(1, z, True)
     attend_hop(0, 1)
     ring_hop(0, 2)
-    ring_start(1, g1)
-    attend(1, z, True)
     attend_hop(0, 2)
-    ring_hop(0, 3)
-    attend_hop(0, 3)
-    ring_hop(1, 1)
-    ring_hop(0, 4)
-    attend_hop(0, 4)
-    attend_hop(1, 1)
-    for hop in range(2, 5):
-        ring_hop(1, hop)
-        attend_hop(1, hop)
+    for c, number in ((1, 1), (0, 3), (1, 2), (0, 4), (1, 3)):
+        ring_hop(c, number)
+        attend_hop(c, number)
+    ring_hop(1, 4)
+    last = lax.rem(z + 4, N_Z)
 
     column = pl.ds(pl.multiple_of(member * HD, HD), HD)
     o_copies = []
     for k in (2, 1, 3, 0):
         index = lax.rem(member + k, GROUP)
         rows = pl.ds(pl.multiple_of(index * PCAP, PCAP), PCAP)
+
+        @pl.when(last < z)
+        def _():
+            attend(1, last, False, (index,))
+
         dead = jnp.sum(jnp.where(diag, live[pl.ds(z * GROUP + index, 1), :], 0.0), axis=1, keepdims=True)
         value = jnp.where(dead < 0, 0.0, mixed[rows, :HD] / mixed[rows, HD:])
         outgoing[k] = (queries[rows, :].astype(F32) + value).astype(BF16)
@@ -406,7 +424,7 @@
     (_, n0), (_, n1) = CHUNKS
     return pl.pallas_call(
         kernel,
-        out_shape=jax.ShapeDtypeStruct((PCAP, COLS), BF16),
+        out_shape=pltpu.VMEM((PCAP, COLS), BF16),
         in_specs=[anywhere, anywhere, anywhere],
         out_specs=pl.BlockSpec(memory_space=pltpu.VMEM),
         scratch_shapes=[
@@ -417,6 +435,7 @@
             pltpu.VMEM((D, 2, COLS), BF16),
             pltpu.VMEM((N_MP, COLS, 2 * COLS), BF16),
             pltpu.VMEM((N_MP, PCAP, COLS), BF16),
+            pltpu.VMEM((PCAP, COLS), BF16),
             pltpu.VMEM((PCAP, 2 * COLS), F32),
             pltpu.VMEM((2, HERE, n0, HD), BF16),
             pltpu.VMEM((2, HERE, n1, HD), BF16),
@@ -429,7 +448,7 @@
             pltpu.VMEM((ROWS, 1), F32),
             pltpu.VMEM((ROWS, 2 * HD), F32),
             pltpu.VMEM((GROUP, PCAP, HD), BF16),
-            dma((3,)), dma, dma, dma((18,)), dma((18,)), dma((3,)), dma((3,)), dma((12,)), dma((12,)),
+            dma((3,)), dma, dma, dma((24,)), dma((24,)), dma((3,)), dma((3,)), dma((12,)), dma((12,)),
             dma((14,)), dma((14,)), dma((14,)), dma((14,)), dma((3,)), dma((3,)),
         ],
         compiler_params=pltpu.CompilerParams(

time: 67.9 us -> 65.9 us (0.971)
  Pallas kernels: 66.2 us -> 65.1 us
  local copies, waits for them, and re-layouts: 1.59 us -> 0.67 us
    pallas_call x1, Pallas kernels: 66.2 us -> 65.1 us  [shards(): pl.pallas_call(kernel, out_shape=pltpu.VMEM((PCAP, COLS), BF16), in_specs...]
    unnamed x1, local copies, waits for them, and re-layouts: 1.59 us -> 0.67 us
where the time goes in v3:
time: 65.9 us; the launch traced here: 65.8 us
  Pallas kernels  65.1 us (99%)
  local copies, waits for them, and re-layouts  0.67 us (1%)
    pallas_call x1, Pallas kernels, shards(): pl.pallas_call(kernel, out_shape=pltpu.VMEM((PCAP, COLS), BF16), in_specs...  65.1 us

profile of v3, /device:TPU:1, one launch (start us, length us, event | category | flops | bytes accessed | tf_op | source)
XLA Modules:
  0.0 65.8 jit_solution(1036920240584126277)
XLA Ops:
  0.0 65.1 %patches.1 = bf16[160,512]{1,0:T(8,128)(2,1)S(1)} custom-call(s32[32,161]{1,0:T(8,128)} %bounds_hbm.1, bf16[3,512,512]{2,1,0:T(8,128)(2,1)} %bitcast.1, bf16[4096,2,512]{2,1,0:T(2,128)(2,1)} %weight_hbm.1), custom_call_target="tpu_custom_call" | custom-call | tf_op jit(solution)/shard_map/patches/pallas_call | solution.py:425
  65.1 0.7 %copy.5 = bf16[160,512]{1,0:T(8,128)(2,1)} copy(bf16[160,512]{1,0:T(8,128)(2,1)S(1)} %patches.1) | data formatting | bytes 327680

commit v4 on v3

--- a/solution.py
+++ b/solution.py
@@ -27,6 +27,7 @@
 F32 = jnp.float32
 BF16 = jnp.bfloat16
 CHUNKS = ((0, 64), (64, 96))
+DIRECT = (0,)
 MESH = pl.DeviceIdType.MESH
 
 
@@ -41,7 +42,7 @@
     bounds_ref, ext, tops, state, weight, plain, states, relay, acc, own0, own1, kv0, kv1,
     queries, live, bias0, bias1, top, mixed, outgoing,
     in_sem, halo_send, halo_recv, mp_send, mp_recv, q_send, q_recv, g_send, g_recv,
-    up_send, up_recv, dn_send, dn_recv, o_send, o_recv,
+    up_send, up_recv, dn_send, dn_recv, o_send, o_recv, d_send, d_recv,
 ):
     ctx = lax.axis_index("ctx")
     mp = lax.axis_index("mp")
@@ -55,6 +56,9 @@
     def at_mp(yy, xx):
         return lax.rem(yy + 4, 4) * 2 + xx
 
+    def owner(plane, k):
+        return lax.rem(plane + N_Z, N_Z) * GROUP + lax.rem(member + k, GROUP)
+
     def mate(k):
         return z * GROUP + lax.rem(member + k, GROUP)
 
@@ -78,6 +82,7 @@
                 {"ctx": ctx, "mp": y_up}, {"ctx": ctx, "mp": y_dn}, {"ctx": mate(2), "mp": x_other},
                 {"ctx": z_up, "mp": mp}, {"ctx": z_dn, "mp": mp}]
     partners += [{"ctx": mate(k), "mp": mp} for k in range(1, GROUP)]
+    partners += [{"ctx": owner(plane, k), "mp": mp} for plane in (z + 1, z - 1) for k in range(1, GROUP)]
     for partner in partners:
         pl.semaphore_signal(barrier, inc=1, device_id=partner, device_id_type=MESH)
     pl.semaphore_wait(barrier, len(partners))
@@ -214,6 +219,11 @@
         else:
             acc[rows, :] += part
 
+    def straight(c, block, part, k, way, src, rows):
+        slot = 16 * c + 8 * way + 4 * part + k
+        to = {"ctx": owner(z - 1 if way else z + 1, k), "mp": mp}
+        return remote(src, kvs[c].at[block, part, rows], d_send.at[slot], d_recv.at[slot], to)
+
     def exchange(c):
         off, count = CHUNKS[c]
         own, kv = owns[c], kvs[c]
@@ -224,6 +234,12 @@
                 own[part, n] = acc[off : off + count, begin : begin + HD].astype(BF16)
         copies = []
         for part in range(2):
+            if c in DIRECT:
+                for k in (1, 2, 3, 0):
+                    for way in range(2):
+                        copy = straight(c, z, part, k, way, own.at[part, lax.rem(member + k, GROUP)], mine)
+                        copy.start()
+                        sent.append(copy)
             for k in range(1, GROUP):
                 slot = 6 * c + part * 3 + k - 1
                 copy = remote(
@@ -252,8 +268,9 @@
         for part in range(2):
             for k in range(3):
                 copies[part * 3 + k].wait_recv()
-            ring_send(c, z, part, part, True)
-            ring_send(c, z, part, part, False)
+            if c not in DIRECT:
+                ring_send(c, z, part, part, True)
+                ring_send(c, z, part, part, False)
 
     def ring_hop(c, hop):
         for part in range(2):
@@ -262,7 +279,16 @@
                 if hop == 4 and part == (1 if up else 0):
                     continue
                 slot = 2 * (hop - 1) + part if hop < 4 else 6
-                piece(c, block, part, slot, up).wait_recv()
+                if hop == 1 and c in DIRECT:
+                    from_plane = lax.rem(block + N_Z, N_Z)
+                    count = CHUNKS[c][1]
+                    for k in range(GROUP):
+                        first = lax.rem(member + GROUP - k, GROUP) * count
+                        rows = pl.ds(pl.multiple_of(first, count), count)
+                        ref = kvs[c].at[from_plane, part, rows]
+                        straight(c, from_plane, part, k, 0 if up else 1, ref, rows).wait_recv()
+                else:
+                    piece(c, block, part, slot, up).wait_recv()
                 if hop < 3:
                     ring_send(c, block, part, 2 * hop + part, up)
                 elif hop == 3 and part == (0 if up else 1):
@@ -343,6 +369,15 @@
     near(1)
     for block in (far, o_dn, o_up, o_far):
         prepare(block)
+
+    bounds = bounds_ref[...]
+    live[...] = jnp.where(bounds[:, 1 : PCAP + 1] > bounds[:, :PCAP], 0.0, MASKED)
+    for c, (off, count) in enumerate(CHUNKS):
+        for block in range(N_Z):
+            biases[c][block : block + 1, :] = jnp.concatenate(
+                [live[block * GROUP + i : block * GROUP + i + 1, off : off + count] for i in range(GROUP)],
+                axis=1,
+            )
     arrived(0, far, 0, 3)
     arrived(0, far, 1, 4)
     project(0, far)
@@ -356,21 +391,15 @@
     g0 = exchange(0)
     for n, block in enumerate((mp, y_dn, y_up, x_other)):
         project(1, block, n == 0)
-    across_near(1)
     arrived(1, far, 0, 3)
     arrived(1, far, 1, 4)
-    for block in (far, o_dn, o_up):
-        project(1, block)
-    ring_start(0, g0)
-
-    bounds = bounds_ref[...]
-    live[...] = jnp.where(bounds[:, 1 : PCAP + 1] > bounds[:, :PCAP], 0.0, MASKED)
-    for c, (off, count) in enumerate(CHUNKS):
-        for block in range(N_Z):
-            biases[c][block : block + 1, :] = jnp.concatenate(
-                [live[block * GROUP + i : block * GROUP + i + 1, off : off + count] for i in range(GROUP)],
-                axis=1,
-            )
+    project(1, far)
+    if 0 not in DIRECT:
+        ring_start(0, g0)
+    across_near(1)
+    project(1, o_dn)
+    project(1, o_up)
+
     arrived(1, o_far, 0, 7)
     arrived(1, o_far, 1, 8)
     project(1, o_far)
@@ -378,6 +407,8 @@
     ring_hop(0, 1)
     for copy in q_copies:
         copy.wait_recv()
+    if 0 in DIRECT:
+        ring_start(0, g0)
     attend(0, z, True)
     ring_start(1, g1)
     attend(1, z, True)
@@ -449,7 +480,7 @@
             pltpu.VMEM((ROWS, 2 * HD), F32),
             pltpu.VMEM((GROUP, PCAP, HD), BF16),
             dma((3,)), dma, dma, dma((24,)), dma((24,)), dma((3,)), dma((3,)), dma((12,)), dma((12,)),
-            dma((14,)), dma((14,)), dma((14,)), dma((14,)), dma((3,)), dma((3,)),
+            dma((14,)), dma((14,)), dma((14,)), dma((14,)), dma((3,)), dma((3,)), dma((32,)), dma((32,)),
         ],
         compiler_params=pltpu.CompilerParams(
             vmem_limit_bytes=60 * 2**20, collective_id=0, has_side_effects=True

time: 65.9 us -> 64.8 us (0.983)
  Pallas kernels: 65.1 us -> 64.1 us
    pallas_call x1, Pallas kernels: 65.1 us -> 64.1 us  [shards(): pl.pallas_call(kernel, out_shape=pltpu.VMEM((PCAP, COLS), BF16), in_specs...]
where the time goes in v4:
time: 64.8 us
  Pallas kernels  64.1 us (99%)
  local copies, waits for them, and re-layouts  0.67 us (1%)
    pallas_call x1, Pallas kernels, shards(): pl.pallas_call(kernel, out_shape=pltpu.VMEM((PCAP, COLS), BF16), in_specs...  64.1 us

profile of v4, /device:TPU:1, one launch (start us, length us, event | category | flops | bytes accessed | tf_op | source)
XLA Modules:
  0.0 64.8 jit_solution(3067503067347197589)
XLA Ops:
  0.0 64.1 %patches.1 = bf16[160,512]{1,0:T(8,128)(2,1)S(1)} custom-call(s32[32,161]{1,0:T(8,128)} %bounds_hbm.1, bf16[3,512,512]{2,1,0:T(8,128)(2,1)} %bitcast.1, bf16[4096,2,512]{2,1,0:T(2,128)(2,1)} %weight_hbm.1), custom_call_target="tpu_custom_call" | custom-call | tf_op jit(solution)/shard_map/patches/pallas_call | solution.py:456
  64.1 0.7 %copy.5 = bf16[160,512]{1,0:T(8,128)(2,1)} copy(bf16[160,512]{1,0:T(8,128)(2,1)S(1)} %patches.1) | data formatting | bytes 327680

commit v5 on v4

--- a/solution.py
+++ b/solution.py
@@ -26,7 +26,7 @@
 MASKED = -1e30
 F32 = jnp.float32
 BF16 = jnp.bfloat16
-CHUNKS = ((0, 64), (64, 96))
+CHUNKS = ((0, 96), (96, 64))
 DIRECT = (0,)
 MESH = pl.DeviceIdType.MESH
 
@@ -130,17 +130,13 @@
         for h in range(HERE):
             cols = slice(h * HD, (h + 1) * HD)
             query = jnp.dot(first, tops[:, cols], preferred_element_type=F32).astype(BF16)
-            scores = (
-                lax.dot_general(
-                    query, ext[1, :, cols], (((1,), (1,)), ((), ())), preferred_element_type=F32
-                )
-                * SCALE
+            scores = lax.dot_general(
+                query, ext[1, :, cols], (((1,), (1,)), ((), ())), preferred_element_type=F32
             )
             scores = jnp.where(inside, scores, MASKED)
-            scores = scores - jnp.max(scores, axis=1, keepdims=True)
-            terms = jnp.where(inside, jnp.exp(scores), 0.0)
-            total = jnp.sum(terms, axis=1, keepdims=True)
-            weights = (terms / jnp.where(total > 0, total, 1.0)).astype(BF16)
+            terms = jnp.exp2((scores - jnp.max(scores, axis=1, keepdims=True)) * SCALE2)
+            factor = jnp.where(end > begin, 1.0 / jnp.sum(terms, axis=1, keepdims=True), 0.0)
+            weights = (terms * factor).astype(BF16)
             state[off : off + count, cols] = jnp.dot(
                 weights, ext[2, :, cols], preferred_element_type=F32
             ).astype(BF16)

time: 64.8 us -> 64.4 us (level)
  no operation moved by 1% of the time
where the time goes in v5:
time: 64.4 us
  Pallas kernels  63.7 us (99%)
  local copies, waits for them, and re-layouts  0.67 us (1%)
    pallas_call x1, Pallas kernels, shards(): pl.pallas_call(kernel, out_shape=pltpu.VMEM((PCAP, COLS), BF16), in_specs...  63.7 us

profile of v5, /device:TPU:1, one launch (start us, length us, event | category | flops | bytes accessed | tf_op | source)
XLA Modules:
  0.0 64.4 jit_solution(8066385694455507701)
XLA Ops:
  0.0 63.7 %patches.1 = bf16[160,512]{1,0:T(8,128)(2,1)S(1)} custom-call(s32[32,161]{1,0:T(8,128)} %bounds_hbm.1, bf16[3,512,512]{2,1,0:T(8,128)(2,1)} %bitcast.1, bf16[4096,2,512]{2,1,0:T(2,128)(2,1)} %weight_hbm.1), custom_call_target="tpu_custom_call" | custom-call | tf_op jit(solution)/shard_map/patches/pallas_call | solution.py:452
  63.7 0.7 %copy.5 = bf16[160,512]{1,0:T(8,128)(2,1)} copy(bf16[160,512]{1,0:T(8,128)(2,1)S(1)} %patches.1) | data formatting | bytes 327680

commit v6 on v5

--- a/solution.py
+++ b/solution.py
@@ -229,13 +229,14 @@
                 begin = part * COLS + n * HD
                 own[part, n] = acc[off : off + count, begin : begin + HD].astype(BF16)
         copies = []
-        for part in range(2):
-            if c in DIRECT:
+        if c in DIRECT:
+            for part in range(2):
                 for k in (1, 2, 3, 0):
                     for way in range(2):
                         copy = straight(c, z, part, k, way, own.at[part, lax.rem(member + k, GROUP)], mine)
                         copy.start()
                         sent.append(copy)
+        for part in range(2):
             for k in range(1, GROUP):
                 slot = 6 * c + part * 3 + k - 1
                 copy = remote(

time: 64.4 us -> 64.4 us (level)
  no operation moved by 1% of the time
where the time goes in v6:
time: 64.4 us
  Pallas kernels  63.7 us (99%)
  local copies, waits for them, and re-layouts  0.67 us (1%)
    pallas_call x1, Pallas kernels, shards(): pl.pallas_call(kernel, out_shape=pltpu.VMEM((PCAP, COLS), BF16), in_specs...  63.7 us

profile of v6, /device:TPU:1, one launch (start us, length us, event | category | flops | bytes accessed | tf_op | source)
XLA Modules:
  0.0 64.4 jit_solution(16263938031638327364)
XLA Ops:
  0.0 63.7 %patches.1 = bf16[160,512]{1,0:T(8,128)(2,1)S(1)} custom-call(s32[32,161]{1,0:T(8,128)} %bounds_hbm.1, bf16[3,512,512]{2,1,0:T(8,128)(2,1)} %bitcast.1, bf16[4096,2,512]{2,1,0:T(2,128)(2,1)} %weight_hbm.1), custom_call_target="tpu_custom_call" | custom-call | tf_op jit(solution)/shard_map/patches/pallas_call | solution.py:453
  63.7 0.7 %copy.5 = bf16[160,512]{1,0:T(8,128)(2,1)} copy(bf16[160,512]{1,0:T(8,128)(2,1)S(1)} %patches.1) | data formatting | bytes 327680
